TPU v7x, 32 devices: a whole 2x2x4 slice. The times are simulated.
32 devices in a mesh: ctx: 8 (over z, x), ch: 4 (over y, core).
Axes of the slice: x: 2, y: 2, z: 4, core: 2. Of those that a mesh axis runs over, the one named last changes fastest.
Arguments:
- signal: float32 [64, 65536], P('ch', 'ctx'), parts along dimension 0, may hold values from -6 to 6
- gate: float32 [64, 65536], P('ch', 'ctx'), parts along dimension 0, may hold values from -6 to 6
- skip: float32 [64], P('ch'), parts along dimension 0, may hold values from 0.5 to 1.5
- filter_spectrum: float32 [16, 2, 64, 8192], P('ctx', None, 'ch'), parts along dimension 2, may hold values from -6 to 6
Outputs:
- gated: float32 [64, 65536], P('ch', 'ctx'), parts along dimension 0
There are 4 independent parts, one for each index of `ch`. A program takes and returns all parts, laid end to end along the dimension named above; each array names one. Nothing has to cross between parts.
All inputs are finite; a program needn't handle non-finite values.
Results may differ from a plain program's by a relative error of at most 0.00005.
Values sent between devices are 32-bit elements; how exact they have to be, the bound alone decides.
No kernel may reach another device: no remote copies, remote signals or barrier semaphores. Data moves between devices by JAX's collectives and lax.ppermute only.
A program may use at most 128 MiB of HBM per device.

v0:
```python
import functools
import math

import jax
import jax.numpy as jnp
import numpy as np
from jax import lax
from jax.experimental import pallas as pl
from jax.experimental.pallas import tpu as pltpu
from jax.sharding import PartitionSpec as P


LANES = 128
HALF = LANES // 2


def split_pair(values):
    high = values.astype(jnp.bfloat16)
    low = (values - high.astype(jnp.float32)).astype(jnp.bfloat16)
    return high, low


def split_table(table):
    table = np.asarray(table, np.float32)
    high = table.astype(jnp.bfloat16)
    low = (table - high.astype(np.float32)).astype(jnp.bfloat16)
    return np.stack([high, low])


def multiply(left, right, dims):
    def dot(a, b):
        return lax.dot_general(a, b, (dims, ((), ())), preferred_element_type=jnp.float32)

    return dot(left[0], right[0]) + (dot(left[0], right[1]) + dot(left[1], right[0]))


def multiply_rows(left, right):
    _, rows, depth = left.shape
    both = jnp.dot(left.reshape(2 * rows, depth), right[0], preferred_element_type=jnp.float32)
    cross = jnp.dot(left[0], right[1], preferred_element_type=jnp.float32)
    return both[:rows] + (both[rows:] + cross)


ROWS_COLS = ((1,), (0,))
COLS_COLS = ((0,), (0,))


@functools.lru_cache(maxsize=None)
def tables(parts, blocks):
    freq_rows = 2 * parts
    period = freq_rows * blocks
    full_len = period * LANES
    rows = np.arange(parts * blocks)
    index = np.zeros((parts, blocks), np.int64)
    for owner in range(parts):
        for place in range(blocks):
            if owner:
                index[owner, place] = freq_rows * place + owner
            elif place < blocks // 2:
                index[owner, place] = freq_rows * place
            else:
                index[owner, place] = freq_rows * place + parts
    index = index.reshape(-1)
    angle = 2 * np.pi * ((index[:, None] * rows[None, :]) % period) / period
    wave_re, wave_im = np.cos(angle), -np.sin(angle)
    wave_im[0] = np.where(rows % 2 == 0, 1.0, -1.0)
    outer = np.stack([wave_re.reshape(-1, LANES, rows.size), wave_im.reshape(-1, LANES, rows.size)], axis=1)
    outer = outer.reshape(-1, rows.size)
    lane = np.arange(LANES)
    turn = 2 * np.pi * ((index[:, None] * lane[None, :]) % full_len) / full_len
    twist = np.stack([np.cos(turn), np.sin(turn)])
    twist[0, 0], twist[1, 0] = 1.0, 0.0
    freq = 2 * (lane % HALF) + lane // HALF
    theta = 2 * np.pi * ((lane[:, None] * freq[None, :]) % LANES) / LANES
    cos, sin = np.cos(theta), np.sin(theta)
    inner = np.block([[cos, -sin], [sin, cos]])
    inner_back = np.block([[cos.T, sin.T], [-sin.T, cos.T]]) / full_len
    upper = lane % HALF >= HALF // 2
    half_theta = 2 * np.pi * ((lane[:, None] * (2 * freq[None, :] + 1)) % (2 * LANES)) / (2 * LANES)
    alternate = np.where(lane % 2 == 0, 1.0, -1.0)
    zero_re, zero_im = np.where(upper, 0.0, cos), np.where(upper, 0.0, -sin)
    zero_re[:, 0], zero_im[:, 0] = 1.0, alternate
    mid_re = np.where(upper, np.cos(half_theta), 0.0)
    mid_im = np.where(upper, -np.sin(half_theta), 0.0)
    edge = np.block([[zero_re, zero_im], [mid_re, mid_im]])
    weight = np.ones(LANES)
    weight[0] = 0.5
    back_re = np.concatenate([(zero_re * weight).T, mid_re.T], axis=1)
    back_im = np.concatenate([(zero_im * weight).T, mid_im.T], axis=1)
    edge_back = np.concatenate([back_re, back_im], axis=0) / full_len
    return {
        "outer": split_table(outer.T),
        "twist": twist.astype(np.float32),
        "there": np.concatenate([split_table(inner), split_table(edge)]),
        "back": np.concatenate([split_table(inner_back), split_table(edge_back)]),
    }


def spread_kernel(device_ref, signal_ref, *refs):
    *out_refs, work_ref = refs
    channels, length = signal_ref.shape
    blocks = length // LANES
    for block in range(blocks):
        work_ref[pl.ds(block, channels, stride=blocks), :] = signal_ref[:, block * LANES : (block + 1) * LANES]
    rows = channels * blocks // len(out_refs)
    for step, out_ref in enumerate(out_refs):
        out_ref[...] = work_ref[part_rows(device_ref, step, rows), :]


def part_rows(device_ref, step, rows):
    return pl.ds(pl.multiple_of((device_ref[0] ^ step) * rows, rows), rows)


def fold_kernel(device_ref, filter_ref, *refs):
    *out_refs, work_ref = refs
    channels = filter_ref.shape[2]
    blocks = filter_ref.shape[3] // LANES
    lane = lax.broadcasted_iota(jnp.int32, (channels, LANES), 1)
    place = lane % HALF
    reverse = LANES - 1 - lane
    negate = jnp.where(place < HALF // 2, LANES - lane, reverse)
    negate_low = jnp.where(place == 0, 0, negate)
    negate_high = jnp.where(place == 0, LANES - HALF // 2 - lane, negate)

    def tile(row, part, block):
        return filter_ref[row, part, :, block * LANES : (block + 1) * LANES]

    def pick(values, where):
        return jnp.take_along_axis(values, where, axis=1)

    def put(part, block, values):
        work_ref[part, pl.ds(block, channels, stride=blocks), :] = values

    @pl.when(device_ref[0] != 0)
    def _():
        for block in range(blocks):
            mirror = blocks - 1 - block
            put(0, block, tile(0, 0, block) + pick(tile(1, 0, mirror), reverse))
            put(1, block, tile(0, 1, block) - pick(tile(1, 1, mirror), reverse))

    @pl.when(device_ref[0] == 0)
    def _():
        for part in range(2):
            sign = 1.0 - 2.0 * part
            for block in range(blocks):
                mirror, wrapped = blocks - 1 - block, (blocks - block) % blocks
                low, low_back = tile(0, part, block), tile(0, part, mirror)
                direct = jnp.where(place < HALF // 2, low, tile(1, part, block))
                back = jnp.where(place < HALF // 2, tile(1, part, mirror), low_back)
                if block < blocks // 2:
                    values = direct + sign * pick(back, negate_low)
                    edge = low + sign * jnp.where(lane == 0, tile(0, part, wrapped), low_back)
                    values = jnp.where(place == 0, edge, values)
                else:
                    direct = jnp.where(place == 0, pltpu.roll(low, LANES - HALF // 2, 1), direct)
                    values = direct + sign * pick(back, negate_high)
                if block == 0 and part == 1:
                    values = jnp.where(lane == 0, 2.0 * tile(0, 0, blocks // 2), values)
                put(part, block, values)

    left = lax.broadcasted_iota(jnp.int32, (blocks, LANES), 1) < HALF
    own = channels // len(out_refs)
    for step, out_ref in enumerate(out_refs):
        for c in range(0, own, 2):
            for part in range(2):
                rows = part_rows(device_ref, step, own * blocks)
                turned = work_ref[part, rows, :][c * blocks : (c + 2) * blocks].T
                first, second = turned[:blocks], turned[blocks:]
                out_ref[c, part] = jnp.where(left, first, pltpu.roll(second, HALF, 1))
                out_ref[c + 1, part] = jnp.where(left, pltpu.roll(first, HALF, 1), second)


def forward_kernel(device_ref, *refs, own):
    *x_refs, outer_ref, twist_ref, inner_ref, out_ref, work_ref = refs
    slots = work_ref.shape[0]
    blocks = slots // len(x_refs)
    for step, x_ref in enumerate(x_refs):
        rows = part_rows(device_ref, step, blocks)
        for c in range(own):
            work_ref[rows, c * LANES : (c + 1) * LANES] = x_ref[c * blocks : (c + 1) * blocks]
    first = multiply((outer_ref[0], outer_ref[1]), split_pair(work_ref[...]), COLS_COLS)
    head = lax.broadcasted_iota(jnp.int32, (8, 2 * LANES), 0) == 0
    for c in range(own):
        pieces = []
        for start in range(0, slots, LANES):
            cos, sin = twist_ref[0, start : start + LANES], twist_ref[1, start : start + LANES]
            re = first[2 * start : 2 * start + LANES, c * LANES : (c + 1) * LANES]
            im = first[2 * start + LANES : 2 * start + 2 * LANES, c * LANES : (c + 1) * LANES]
            pieces.append(jnp.concatenate([re * cos + im * sin, im * cos - re * sin], axis=1))
        pair = split_pair(jnp.concatenate(pieces, axis=0))
        spectrum = multiply(pair, (inner_ref[0], inner_ref[1]), ROWS_COLS)
        edge = multiply((pair[0][:16], pair[1][:16]), (inner_ref[2], inner_ref[3]), ROWS_COLS)
        out_ref[c, 0] = spectrum[:, :LANES]
        out_ref[c, 1] = spectrum[:, LANES:]
        top = jnp.where(head, edge[:8], spectrum[:8])
        out_ref[c, 0, :8] = top[:, :LANES]
        out_ref[c, 1, :8] = top[:, LANES:]


def backward_kernel(device_ref, spectrum_ref, *refs, steps, parts):
    filter_refs, (outer_ref, twist_ref, inner_ref, *refs) = refs[: len(steps)], refs[len(steps) :]
    *refs, product_ref = refs
    own, _, slots, _ = spectrum_ref.shape
    blocks = slots // parts
    held = blocks * len(steps)
    row = lax.broadcasted_iota(jnp.int32, (blocks, LANES), 0)
    lane = lax.broadcasted_iota(jnp.int32, (blocks, LANES), 1)
    corner_place = jnp.logical_and(row == 0, lane == 0)
    for index, step in enumerate(steps):
        owner = device_ref[0] ^ step
        rows = part_rows(device_ref, step, blocks)
        place = index // 2 * LANES + (owner & 1) * blocks
        place = pl.ds(pl.multiple_of(place, blocks), blocks)
        corner = jnp.logical_and(corner_place, owner == 0)
        for c in range(own):
            filt_re, filt_im = filter_refs[index][c, 0], filter_refs[index][c, 1]
            re, im = spectrum_ref[c, 0, rows, :], spectrum_ref[c, 1, rows, :]
            low, high = re * filt_re, im * filt_im
            out_re = jnp.where(corner, low, low - high)
            out_im = jnp.where(corner, high, re * filt_im + im * filt_re)
            for level, values in enumerate(split_pair(jnp.concatenate([out_re, out_im], axis=1))):
                product_ref[level, c, place, :] = values
    products = product_ref[...].reshape(2, own * held, 2 * LANES)
    spread = multiply_rows(products, (inner_ref[0], inner_ref[1]))
    starts = range(0, held, LANES)
    tops = [product_ref[:, c, start : start + 16] for c in range(own) for start in starts]
    edges = multiply_rows(jnp.concatenate(tops, axis=1), (inner_ref[2], inner_ref[3]))
    head = lax.broadcasted_iota(jnp.int32, (8, 2 * LANES), 0) == 0
    columns, tables = [], []
    for c in range(own):
        pieces = []
        for index, start in enumerate(starts):
            pair = (device_ref[0] ^ steps[2 * index]) // 2
            rows = pl.ds(pl.multiple_of(pair * LANES, LANES), LANES)
            cos, sin = twist_ref[0, rows, :], twist_ref[1, rows, :]
            back = spread[c * held + start : c * held + start + LANES]
            edge = edges[16 * (c * len(starts) + index) :][:8]
            top = jnp.where(jnp.logical_and(head, pair == 0), edge, back[:8])
            back = jnp.concatenate([top, back[8:]], axis=0)
            re, im = back[:, :LANES], back[:, LANES:]
            pieces += [re * cos - im * sin, im * cos + re * sin]
            if c == 0:
                tables.append(outer_ref[:, :, pl.ds(pl.multiple_of(pair * 2 * LANES, 2 * LANES), 2 * LANES)])
        columns.append(jnp.concatenate(pieces, axis=0))
    turned = split_pair(jnp.concatenate(columns, axis=1))
    total = multiply_rows(jnp.concatenate(tables, axis=2), turned)
    if len(refs) == 1:
        refs[0][...] = total
        return
    sum_ref, *out_refs, work_ref = refs
    work_ref[...] = sum_ref[...] + total
    for step, out_ref in enumerate(out_refs):
        rows = part_rows(device_ref, step, blocks)
        for c in range(own):
            out_ref[c * blocks : (c + 1) * blocks] = work_ref[rows, c * LANES : (c + 1) * LANES]


def split_steps(parts):
    early = [step for step in range(parts) if step & 2 == 0]
    return early, [step for step in range(parts) if step & 2]


def ready_kernel(skip_ref, signal_ref, gate_ref, scale_ref, base_ref):
    channels, length = signal_ref.shape
    row = lax.broadcasted_iota(jnp.int32, (channels, LANES), 0)
    skip = jnp.zeros((channels, LANES), jnp.float32)
    for channel in range(channels):
        skip = jnp.where(row == channel, skip_ref[channel], skip)
    for start in range(0, length, LANES):
        where = slice(start, start + LANES)
        gate = gate_ref[:, where]
        scale_ref[:, where] = gate
        base_ref[:, where] = gate * (skip * signal_ref[:, where])


def finish_kernel(device_ref, *refs):
    *conv_refs, scale_ref, base_ref, out_ref, work_ref = refs
    channels, length = base_ref.shape
    blocks = length // LANES
    for step, conv_ref in enumerate(conv_refs):
        work_ref[part_rows(device_ref, step, conv_ref.shape[0]), :] = conv_ref[...]
    for block in range(blocks):
        where = slice(block * LANES, (block + 1) * LANES)
        conv = work_ref[pl.ds(block, channels, stride=blocks), :]
        out_ref[:, where] = scale_ref[:, where] * conv + base_ref[:, where]


def call(kernel, shapes, device, *operands, scratch, limit):
    one = not isinstance(shapes, list)
    shapes = [shapes] if one else shapes
    vmem = pl.BlockSpec(memory_space=pltpu.VMEM)
    run = pl.pallas_call(
        kernel,
        out_shape=[jax.ShapeDtypeStruct(shape, jnp.float32) for shape in shapes],
        in_specs=[pl.BlockSpec(memory_space=pltpu.SMEM)] + [vmem] * len(operands),
        out_specs=[vmem] * len(shapes),
        scratch_shapes=scratch,
        compiler_params=pltpu.CompilerParams(vmem_limit_bytes=limit << 20),
    )
    result = run(device, *operands)
    return result[0] if one else result


def exchange(blocks):
    parts = len(blocks)
    moved = [None] * parts
    moved[0] = blocks[0]
    for step in range(1, parts):
        moved[step] = lax.ppermute(blocks[step], "ctx", [(one, one ^ step) for one in range(parts)])
    return moved


def by_channel(signal, gate, skip, filter_spectrum):
    parts = lax.axis_size("ctx")
    channels, length = signal.shape
    blocks, own = length // LANES, channels // parts
    slots = parts * blocks
    table = tables(parts, blocks)
    device = lax.axis_index("ctx")[None]
    piece = (own * blocks, LANES)
    whole = pltpu.VMEM((channels * blocks, LANES), jnp.float32)
    spread = call(spread_kernel, [piece] * parts, device, signal, scratch=[whole], limit=4)
    columns = exchange(spread)
    scale, base = call(ready_kernel, [signal.shape] * 2, skip, signal, gate, scratch=[], limit=6)
    folded = call(
        fold_kernel,
        [(own, 2, blocks, LANES)] * parts,
        device,
        filter_spectrum,
        scratch=[pltpu.VMEM((2, channels * blocks, LANES), jnp.float32)],
        limit=10,
    )
    filt = exchange(folded)
    spectrum = call(
        functools.partial(forward_kernel, own=own),
        (own, 2, slots, LANES),
        device,
        *columns,
        table["outer"],
        table["twist"],
        table["there"],
        scratch=[pltpu.VMEM((slots, own * LANES), jnp.float32)],
        limit=12,
    )
    back_tables = (table["outer"], table["twist"], table["back"])
    early, late = split_steps(parts)
    product = pltpu.VMEM((2, own, slots // 2, 2 * LANES), jnp.bfloat16)
    partial = call(
        functools.partial(backward_kernel, steps=early, parts=parts),
        (slots, own * LANES),
        device,
        spectrum,
        *[filt[step] for step in early],
        *back_tables,
        scratch=[product],
        limit=10,
    )
    rows = call(
        functools.partial(backward_kernel, steps=late, parts=parts),
        [piece] * parts,
        device,
        spectrum,
        *[filt[step] for step in late],
        *back_tables,
        partial,
        scratch=[pltpu.VMEM((slots, own * LANES), jnp.float32), product],
        limit=10,
    )
    convolved = exchange(rows)
    return call(finish_kernel, signal.shape, device, *convolved, scale, base, scratch=[whole], limit=6)


def contract(form, left, right):
    return jnp.einsum(form, left, right, precision=lax.Precision.HIGHEST)


def phase_table(left, right, period):
    angle = left * right % period
    theta = angle.astype(jnp.float32) * (2.0 * math.pi / period)
    return (jnp.cos(theta), jnp.sin(theta))


def product_pair(form, left, right):
    real_part = contract(form, left[0], right[0]) - contract(form, left[1], right[1])
    imag_part = contract(form, left[0], right[1]) + contract(form, left[1], right[0])
    return (real_part, imag_part)


def times_pair(left, right):
    return (left[0] * right[0] - left[1] * right[1], left[0] * right[1] + left[1] * right[0])


def local_tables(length):
    outer_len = 128
    inner_len = length // outer_len
    outer_index = jnp.arange(outer_len, dtype=jnp.int32)
    inner_index = jnp.arange(inner_len, dtype=jnp.int32)
    outer_wave = phase_table(outer_index[:, None], outer_index[None, :], outer_len)
    twist_wave = phase_table(outer_index[:, None], inner_index[None, :], length)
    inner_wave = phase_table(inner_index[:, None], inner_index[None, :], inner_len)
    return (outer_len, inner_len, outer_wave, twist_wave, inner_wave)


def local_forward(values, length):
    outer_len, inner_len, outer_wave, twist_wave, inner_wave = local_tables(length)
    lead_shape = values[0].shape[:-1]
    values = tuple((part.reshape(lead_shape + (outer_len, inner_len)) for part in values))
    values = product_pair("as,...sb->...ab", (outer_wave[0], -outer_wave[1]), values)
    values = times_pair(values, (twist_wave[0], -twist_wave[1]))
    return product_pair("...as,bs->...ab", values, (inner_wave[0], -inner_wave[1]))


def local_inverse(values, length):
    _, _, outer_wave, twist_wave, inner_wave = local_tables(length)
    lead_shape = values[0].shape[:-2]
    values = product_pair("...ak,sk->...as", values, inner_wave)
    values = times_pair(values, twist_wave)
    values = product_pair("ta,...as->...ts", outer_wave, values)
    return tuple((part.reshape(lead_shape + (length,)) for part in values))


def by_frequency(signal, gate, skip, filter_spectrum):
    parts_count = lax.axis_size("ctx")
    freq_rows = 2 * parts_count
    channels, tok_local = signal.shape
    slice_len = tok_local // parts_count
    full_len = freq_rows * tok_local
    device = lax.axis_index("ctx")
    is_first = device == 0
    columns = lax.all_to_all(signal[None], "ctx", split_axis=2, concat_axis=0, tiled=True)
    source_row = jnp.arange(parts_count, dtype=jnp.int32)
    dest_index = jnp.arange(parts_count, dtype=jnp.int32)
    slice_pos = device * slice_len + jnp.arange(slice_len, dtype=jnp.int32)
    upper_freq = jnp.where(dest_index == 0, parts_count, freq_rows - dest_index)
    row_freq = jnp.stack([dest_index, upper_freq], axis=1).reshape(freq_rows)
    spot = jnp.arange(tok_local, dtype=jnp.int32)
    wave_cos, wave_sin = phase_table(row_freq[:, None], source_row[None, :], freq_rows)
    first_re = contract("kr,rcq->kcq", wave_cos, columns)
    first_im = -contract("kr,rcq->kcq", wave_sin, columns)
    twist_cos, twist_sin = phase_table(row_freq[:, None], slice_pos[None, :], full_len)
    first_pair = times_pair((first_re, first_im), (twist_cos[:, None, :], -twist_sin[:, None, :]))
    stacked = jnp.stack(first_pair, axis=1)
    moved = lax.all_to_all(stacked, "ctx", split_axis=0, concat_axis=3, tiled=True)
    low_pair = (moved[0, 0], moved[0, 1])
    high_pair = (moved[1, 0], moved[1, 1])
    rows_pair = (jnp.stack([low_pair[0], high_pair[0]]), jnp.stack([low_pair[1], high_pair[1]]))
    spectral = local_forward(rows_pair, tok_local)
    inner_len = tok_local // 128
    filt = filter_spectrum.reshape(2, 2, channels, inner_len, 128).swapaxes(3, 4)
    product = times_pair(spectral, (filt[:, 0], filt[:, 1]))
    restored = local_inverse(product, tok_local)
    my_freq = jnp.stack([device, jnp.where(is_first, parts_count, freq_rows - device)])
    back_cos, back_sin = phase_table(my_freq[:, None], spot[None, :], full_len)
    turned = times_pair(restored, (back_cos[:, None, :], back_sin[:, None, :]))
    scale_factor = 1.0 / full_len
    stacked = jnp.stack(turned, axis=1)
    moved = lax.all_to_all(stacked, "ctx", split_axis=3, concat_axis=0, tiled=True)
    out_cos, out_sin = phase_table(source_row[:, None], row_freq[None, :], freq_rows)
    rows_all = contract("rm,mcq->rcq", out_cos, moved[:, 0]) - contract(
        "rm,mcq->rcq", out_sin, moved[:, 1]
    )
    rows_all = rows_all * scale_factor
    convolved = lax.all_to_all(rows_all, "ctx", split_axis=0, concat_axis=2, tiled=True)
    return gate * (convolved[0] + skip[:, None] * signal)


def shards(signal, gate, skip, filter_spectrum):
    parts = lax.axis_size("ctx")
    channels, length = signal.shape
    if channels % (2 * parts) == 0 and parts & (parts - 1) == 0 and parts >= 4 and 2 * length == LANES * LANES:
        return by_channel(signal, gate, skip, filter_spectrum)
    return by_frequency(signal, gate, skip, filter_spectrum)


def solution(mesh):
    return jax.shard_map(
        shards,
        mesh=mesh,
        in_specs=(P("ch", "ctx"), P("ch", "ctx"), P("ch"), P("ctx", None, "ch", None)),
        out_specs=P("ch", "ctx"),
        check_vma=False,
    )
```

profile of v0, /device:TPU:0, one launch (start us, length us, event | category | flops | bytes accessed | tf_op | source)
XLA Modules:
  0.0 64.7 jit_solution(17911315721336939906)
XLA Ops:
  0.0 1.2 %copy-done.3 = f32[16,8192]{1,0:T(8,128)S(1)} copy-done((f32[16,8192]{1,0:T(8,128)S(1)}, f32[16,8192]{1,0:T(8,128)}, u32[]{:S(2)}) %copy-start.3) | copy-done | bytes 524312
  1.7 3.0 %collective-permute-start = (f32[128,128]{1,0:T(8,128)S(1)}, f32[128,128]{1,0:T(8,128)S(1)}, u32[]{:S(2)}, u32[]{:S(2)}) collective-permute-start(f32[128,128]{1,0:T(8,128)S(1)} %get-tuple-element.32), channel_id=1, source_target_pairs={{0,4},{4,0},{8,12},{12,8},{16,20},{20,16},{24,28},{28,24},{1,5},{5... | collective-permute-start | bytes 196616 | tf_op jit(solution)/shard_map/ppermute | solution.py:309
  4.7 1.6 %collective-permute-start.1 = (f32[128,128]{1,0:T(8,128)S(1)}, f32[128,128]{1,0:T(8,128)S(1)}, u32[]{:S(2)}, u32[]{:S(2)}) collective-permute-start(f32[128,128]{1,0:T(8,128)S(1)} %get-tuple-element.33), channel_id=1, source_target_pairs={{0,8},{4,12},{8,0},{12,4},{16,24},{20,28},{24,16},{28,20},{1,9},{5... | collective-permute-start | bytes 196616 | tf_op jit(solution)/shard_map/ppermute | solution.py:309
  6.3 3.0 %collective-permute-start.3 = (f32[128,128]{1,0:T(8,128)S(1)}, f32[128,128]{1,0:T(8,128)S(1)}, u32[]{:S(2)}, u32[]{:S(2)}) collective-permute-start(f32[128,128]{1,0:T(8,128)S(1)} %get-tuple-element.35), channel_id=1, source_target_pairs={{0,16},{4,20},{8,24},{12,28},{16,0},{20,4},{24,8},{28,12},{1,17},{... | collective-permute-start | bytes 196616 | tf_op jit(solution)/shard_map/ppermute | solution.py:309
  9.3 1.6 %copy-done.2 = f32[2,2,16,8192]{3,2,1,0:T(8,128)S(1)} copy-done((f32[2,2,16,8192]{3,2,1,0:T(8,128)S(1)}, f32[2,2,16,8192]{3,2,1,0:T(8,128)}, u32[]{:S(2)}) %copy-start.2) | copy-done | bytes 2097176
  10.9 1.6 %shard_map.84 = (f32[2,2,64,128]{3,2,1,0:T(8,128)S(1)}, f32[2,2,64,128]{3,2,1,0:T(8,128)S(1)}, f32[2,2,64,128]{3,2,1,0:T(8,128)S(1)}, f32[2,2,64,128]{3,2,1,0:T(...) custom-call(s32[1]{0:T(128)} %bitcast.device_ref, ...), custom_call_target="tpu_custom_call" | custom-call | tf_op jit(solution)/shard_map/pallas_call | solution.py:300
  12.5 1.7 %collective-permute-start.11 = (f32[2,2,64,128]{3,2,1,0:T(8,128)S(1)}, f32[2,2,64,128]{3,2,1,0:T(8,128)S(1)}, u32[]{:S(2)}, u32[]{:S(2)}) collective-permute-start(f32[2,2,64,128]{3,2,1,0:T(8,128)S(1)} %get-tuple-element.44), channel_id=1, source_target_pairs={{0,4},{4,0},{8,12},{12,8},{16,20},{20,16},{24,28},{28,24},{1,5},{5... | collective-permute-start | bytes 393224 | tf_op jit(solution)/shard_map/ppermute | solution.py:309
  14.5 2.4 %collective-permute-start.4 = (f32[128,128]{1,0:T(8,128)S(1)}, f32[128,128]{1,0:T(8,128)S(1)}, u32[]{:S(2)}, u32[]{:S(2)}) collective-permute-start(f32[128,128]{1,0:T(8,128)S(1)} %get-tuple-element.36), channel_id=1, source_target_pairs={{0,20},{4,16},{8,28},{12,24},{16,4},{20,0},{24,12},{28,8},{1,21},{... | collective-permute-start | bytes 196616 | tf_op jit(solution)/shard_map/ppermute | solution.py:309
  16.9 1.5 %collective-permute-start.5 = (f32[128,128]{1,0:T(8,128)S(1)}, f32[128,128]{1,0:T(8,128)S(1)}, u32[]{:S(2)}, u32[]{:S(2)}) collective-permute-start(f32[128,128]{1,0:T(8,128)S(1)} %get-tuple-element.37), channel_id=1, source_target_pairs={{0,24},{4,28},{8,16},{12,20},{16,8},{20,12},{24,0},{28,4},{1,25},{... | collective-permute-start | bytes 196616 | tf_op jit(solution)/shard_map/ppermute | solution.py:309
  18.4 3.4 %collective-permute-start.6 = (f32[128,128]{1,0:T(8,128)S(1)}, f32[128,128]{1,0:T(8,128)S(1)}, u32[]{:S(2)}, u32[]{:S(2)}) collective-permute-start(f32[128,128]{1,0:T(8,128)S(1)} %get-tuple-element.38), channel_id=1, source_target_pairs={{0,28},{4,24},{8,20},{12,16},{16,12},{20,8},{24,4},{28,0},{1,29},{... | collective-permute-start | bytes 196616 | tf_op jit(solution)/shard_map/ppermute | solution.py:309
  21.9 6.6 %collective-permute-done.4.refs_5_ = f32[128,128]{1,0:T(8,128)S(1)} collective-permute-done((f32[128,128]{1,0:T(8,128)S(1)}, f32[128,128]{1,0:T(8,128)S(1)}, u32[]{:S(2)}, u32[]{:S(2)}) %collective-permute-start.4) | collective-permute-done | bytes 65568 | tf_op jit(solution)/shard_map/ppermute | solution.py:309
  28.4 2.4 %collective-permute-start.13 = (f32[2,2,64,128]{3,2,1,0:T(8,128)S(1)}, f32[2,2,64,128]{3,2,1,0:T(8,128)S(1)}, u32[]{:S(2)}, u32[]{:S(2)}) collective-permute-start(f32[2,2,64,128]{3,2,1,0:T(8,128)S(1)} %get-tuple-element.46), channel_id=1, source_target_pairs={{0,20},{4,16},{8,28},{12,24},{16,4},{20,0},{24,12},{28,8},{1,21},{... | collective-permute-start | bytes 393224 | tf_op jit(solution)/shard_map/ppermute | solution.py:309
  30.9 0.8 %collective-permute-start.8 = (f32[2,2,64,128]{3,2,1,0:T(8,128)S(1)}, f32[2,2,64,128]{3,2,1,0:T(8,128)S(1)}, u32[]{:S(2)}, u32[]{:S(2)}) collective-permute-start(f32[2,2,64,128]{3,2,1,0:T(8,128)S(1)} %get-tuple-element.40), channel_id=1, source_target_pairs={{0,12},{4,8},{8,4},{12,0},{16,28},{20,24},{24,20},{28,16},{1,13},{... | collective-permute-start | bytes 393224 | tf_op jit(solution)/shard_map/ppermute | solution.py:309
  31.6 2.2 %collective-permute-start.9 = (f32[2,2,64,128]{3,2,1,0:T(8,128)S(1)}, f32[2,2,64,128]{3,2,1,0:T(8,128)S(1)}, u32[]{:S(2)}, u32[]{:S(2)}) collective-permute-start(f32[2,2,64,128]{3,2,1,0:T(8,128)S(1)} %get-tuple-element.41), channel_id=1, source_target_pairs={{0,24},{4,28},{8,16},{12,20},{16,8},{20,12},{24,0},{28,4},{1,25},{... | collective-permute-start | bytes 393224 | tf_op jit(solution)/shard_map/ppermute | solution.py:309
  33.8 1.8 %collective-permute-start.10 = (f32[2,2,64,128]{3,2,1,0:T(8,128)S(1)}, f32[2,2,64,128]{3,2,1,0:T(8,128)S(1)}, u32[]{:S(2)}, u32[]{:S(2)}) collective-permute-start(f32[2,2,64,128]{3,2,1,0:T(8,128)S(1)} %get-tuple-element.42), channel_id=1, source_target_pairs={{0,28},{4,24},{8,20},{12,16},{16,12},{20,8},{24,4},{28,0},{1,29},{... | collective-permute-start | bytes 393224 | tf_op jit(solution)/shard_map/ppermute | solution.py:309
  35.6 1.0 %copy-done.6 = bf16[4,256,256]{2,1,0:T(8,128)(2,1)S(1)} copy-done((bf16[4,256,256]{2,1,0:T(8,128)(2,1)S(1)}, bf16[4,256,256]{2,1,0:T(8,128)(2,1)}, u32[]{:S(2)}) %copy-start.6) | copy-done | bytes 524312
  36.7 2.5 %shard_map.83.spectrum_ref = f32[2,2,512,128]{3,2,1,0:T(8,128)S(1)} custom-call(s32[1]{0:T(128)} %bitcast.device_ref, f32[128,128]{1,0:T(8,128)S(1)} %get-tuple-element.31.refs_0_, f32[128,128]{1,0:T(8,128)S(1)} %collective-permute-done.refs_1_, f32[128,128]{1,0:T(8,128)S(1)} %collective-permute-done.1.refs_2_, ...), custom_call_target="tpu_custom_call" | custom-call | tf_op jit(solution)/shard_map/pallas_call | solution.py:300
  39.2 0.8 %collective-permute-done.13.refs_3_ = f32[2,2,64,128]{3,2,1,0:T(8,128)S(1)} collective-permute-done((f32[2,2,64,128]{3,2,1,0:T(8,128)S(1)}, f32[2,2,64,128]{3,2,1,0:T(8,128)S(1)}, u32[]{:S(2)}, u32[]{:S(2)}) %collective-permute-start.13) | collective-permute-done | bytes 131104 | tf_op jit(solution)/shard_map/ppermute | solution.py:309
  40.0 1.3 %shard_map.85.refs_7_ = f32[512,256]{1,0:T(8,128)S(1)} custom-call(s32[1]{0:T(128)} %bitcast.device_ref, f32[2,2,512,128]{3,2,1,0:T(8,128)S(1)} %shard_map.83.spectrum_ref, f32[2,2,64,128]{3,2,1,0:T(8,128)S(1)} %get-tuple-element.43.refs_0_, f32[2,2,64,128]{3,2,1,0:T(8,128)S(1)} %collective-permute-done.11.refs_1_, ...), custom_call_target="tpu_custom_call" | custom-call | tf_op jit(solution)/shard_map/pallas_call | solution.py:300
  41.3 1.0 %collective-permute-done.9.refs_2_ = f32[2,2,64,128]{3,2,1,0:T(8,128)S(1)} collective-permute-done((f32[2,2,64,128]{3,2,1,0:T(8,128)S(1)}, f32[2,2,64,128]{3,2,1,0:T(8,128)S(1)}, u32[]{:S(2)}, u32[]{:S(2)}) %collective-permute-start.9) | collective-permute-done | bytes 131104 | tf_op jit(solution)/shard_map/ppermute | solution.py:309
  42.3 2.2 %collective-permute-done.10.refs_3_ = f32[2,2,64,128]{3,2,1,0:T(8,128)S(1)} collective-permute-done((f32[2,2,64,128]{3,2,1,0:T(8,128)S(1)}, f32[2,2,64,128]{3,2,1,0:T(8,128)S(1)}, u32[]{:S(2)}, u32[]{:S(2)}) %collective-permute-start.10) | collective-permute-done | bytes 131104 | tf_op jit(solution)/shard_map/ppermute | solution.py:309
  44.5 1.3 %shard_map.86 = (f32[128,128]{1,0:T(8,128)S(1)}, f32[128,128]{1,0:T(8,128)S(1)}, f32[128,128]{1,0:T(8,128)S(1)}, f32[128,128]{1,0:T(8,128)S(1)}, f32[128,128]{1,...) custom-call(s32[1]{0:T(128)} %bitcast.device_ref, ...), custom_call_target="tpu_custom_call" | custom-call | tf_op jit(solution)/shard_map/pallas_call | solution.py:300
  45.8 2.1 %collective-permute-start.14 = (f32[128,128]{1,0:T(8,128)S(1)}, f32[128,128]{1,0:T(8,128)S(1)}, u32[]{:S(2)}, u32[]{:S(2)}) collective-permute-start(f32[128,128]{1,0:T(8,128)S(1)} %get-tuple-element.48), channel_id=1, source_target_pairs={{0,4},{4,0},{8,12},{12,8},{16,20},{20,16},{24,28},{28,24},{1,5},{5... | collective-permute-start | bytes 196616 | tf_op jit(solution)/shard_map/ppermute | solution.py:309
  48.0 3.0 %collective-permute-start.15 = (f32[128,128]{1,0:T(8,128)S(1)}, f32[128,128]{1,0:T(8,128)S(1)}, u32[]{:S(2)}, u32[]{:S(2)}) collective-permute-start(f32[128,128]{1,0:T(8,128)S(1)} %get-tuple-element.49), channel_id=1, source_target_pairs={{0,8},{4,12},{8,0},{12,4},{16,24},{20,28},{24,16},{28,20},{1,9},{5... | collective-permute-start | bytes 196616 | tf_op jit(solution)/shard_map/ppermute | solution.py:309
  51.2 2.1 %collective-permute-start.17 = (f32[128,128]{1,0:T(8,128)S(1)}, f32[128,128]{1,0:T(8,128)S(1)}, u32[]{:S(2)}, u32[]{:S(2)}) collective-permute-start(f32[128,128]{1,0:T(8,128)S(1)} %get-tuple-element.51), channel_id=1, source_target_pairs={{0,16},{4,20},{8,24},{12,28},{16,0},{20,4},{24,8},{28,12},{1,17},{... | collective-permute-start | bytes 196616 | tf_op jit(solution)/shard_map/ppermute | solution.py:309
  53.3 1.4 %collective-permute-start.18 = (f32[128,128]{1,0:T(8,128)S(1)}, f32[128,128]{1,0:T(8,128)S(1)}, u32[]{:S(2)}, u32[]{:S(2)}) collective-permute-start(f32[128,128]{1,0:T(8,128)S(1)} %get-tuple-element.52), channel_id=1, source_target_pairs={{0,20},{4,16},{8,28},{12,24},{16,4},{20,0},{24,12},{28,8},{1,21},{... | collective-permute-start | bytes 196616 | tf_op jit(solution)/shard_map/ppermute | solution.py:309
  54.8 1.5 %collective-permute-start.19 = (f32[128,128]{1,0:T(8,128)S(1)}, f32[128,128]{1,0:T(8,128)S(1)}, u32[]{:S(2)}, u32[]{:S(2)}) collective-permute-start(f32[128,128]{1,0:T(8,128)S(1)} %get-tuple-element.53), channel_id=1, source_target_pairs={{0,24},{4,28},{8,16},{12,20},{16,8},{20,12},{24,0},{28,4},{1,25},{... | collective-permute-start | bytes 196616 | tf_op jit(solution)/shard_map/ppermute | solution.py:309
  56.2 2.6 %collective-permute-start.20 = (f32[128,128]{1,0:T(8,128)S(1)}, f32[128,128]{1,0:T(8,128)S(1)}, u32[]{:S(2)}, u32[]{:S(2)}) collective-permute-start(f32[128,128]{1,0:T(8,128)S(1)} %get-tuple-element.54), channel_id=1, source_target_pairs={{0,28},{4,24},{8,20},{12,16},{16,12},{20,8},{24,4},{28,0},{1,29},{... | collective-permute-start | bytes 196616 | tf_op jit(solution)/shard_map/ppermute | solution.py:309
  58.9 0.6 shard_map.87
  59.5 0.5 collective-permute-done.17.refs_4_
  60.0 3.4 %collective-permute-done.18.refs_5_ = f32[128,128]{1,0:T(8,128)S(1)} collective-permute-done((f32[128,128]{1,0:T(8,128)S(1)}, f32[128,128]{1,0:T(8,128)S(1)}, u32[]{:S(2)}, u32[]{:S(2)}) %collective-permute-start.18) | collective-permute-done | bytes 65568 | tf_op jit(solution)/shard_map/ppermute | solution.py:309
  63.5 1.2 %shard_map.88 = f32[16,8192]{1,0:T(8,128)} custom-call(s32[1]{0:T(128)} %bitcast.device_ref, f32[128,128]{1,0:T(8,128)S(1)} %get-tuple-element.47.refs_0_, f32[128,128]{1,0:T(8,128)S(1)} %collective-permute-done.14.refs_1_, f32[128,128]{1,0:T(8,128)S(1)} %collective-permute-done.15.refs_2_, f32[128,128]{1,0:T(8,128)S(1)} %collective-permute-done.16.refs_3_, ...), custom_call_target="tpu_custom_call" | custom-call | tf_op jit(solution)/shard_map/pallas_call | solution.py:300
  (35 shorter events, 1.2 us)
Async XLA Ops:
  0.0 35.6 %copy-start.1 = (f32[2,512,128]{2,1,0:T(8,128)S(1)}, f32[2,512,128]{2,1,0:T(8,128)}, u32[]{:S(2)}) copy-start(f32[2,512,128]{2,1,0:T(8,128)} %constant.15.clone.refs_9_.refs_5_) | copy-start | bytes 1572868
  0.0 35.6 %copy-start = (bf16[2,512,1024]{2,1,0:T(8,128)(2,1)S(1)}, bf16[2,512,1024]{2,1,0:T(8,128)(2,1)}, u32[]{:S(2)}) copy-start(bf16[2,512,1024]{2,1,0:T(8,128)(2,1)} %constant.14.clone.refs_8_.refs_4_) | copy-start | bytes 6291460
  0.0 1.2 %copy-start.3 = (f32[16,8192]{1,0:T(8,128)S(1)}, f32[16,8192]{1,0:T(8,128)}, u32[]{:S(2)}) copy-start(f32[16,8192]{1,0:T(8,128)} %signal_ref.3) | copy-start | bytes 1572868
  1.7 12.5 %collective-permute-start = (f32[128,128]{1,0:T(8,128)S(1)}, f32[128,128]{1,0:T(8,128)S(1)}, u32[]{:S(2)}, u32[]{:S(2)}) collective-permute-start(f32[128,128]{1,0:T(8,128)S(1)} %get-tuple-element.32), channel_id=1, source_target_pairs={{0,4},{4,0},{8,12},{12,8},{16,20},{20,16},{24,28},{28,24},{1,5},{5... | collective-permute-start | bytes 196616 | tf_op jit(solution)/shard_map/ppermute | solution.py:309
  4.7 9.8 %collective-permute-start.1 = (f32[128,128]{1,0:T(8,128)S(1)}, f32[128,128]{1,0:T(8,128)S(1)}, u32[]{:S(2)}, u32[]{:S(2)}) collective-permute-start(f32[128,128]{1,0:T(8,128)S(1)} %get-tuple-element.33), channel_id=1, source_target_pairs={{0,8},{4,12},{8,0},{12,4},{16,24},{20,28},{24,16},{28,20},{1,9},{5... | collective-permute-start | bytes 196616 | tf_op jit(solution)/shard_map/ppermute | solution.py:309
  6.3 10.6 %collective-permute-start.2 = (f32[128,128]{1,0:T(8,128)S(1)}, f32[128,128]{1,0:T(8,128)S(1)}, u32[]{:S(2)}, u32[]{:S(2)}) collective-permute-start(f32[128,128]{1,0:T(8,128)S(1)} %get-tuple-element.34), channel_id=1, source_target_pairs={{0,12},{4,8},{8,4},{12,0},{16,28},{20,24},{24,20},{28,16},{1,13},{... | collective-permute-start | bytes 196616 | tf_op jit(solution)/shard_map/ppermute | solution.py:309
  6.3 12.1 %collective-permute-start.3 = (f32[128,128]{1,0:T(8,128)S(1)}, f32[128,128]{1,0:T(8,128)S(1)}, u32[]{:S(2)}, u32[]{:S(2)}) collective-permute-start(f32[128,128]{1,0:T(8,128)S(1)} %get-tuple-element.35), channel_id=1, source_target_pairs={{0,16},{4,20},{8,24},{12,28},{16,0},{20,4},{24,8},{28,12},{1,17},{... | collective-permute-start | bytes 196616 | tf_op jit(solution)/shard_map/ppermute | solution.py:309
  9.3 1.6 %copy-start.2 = (f32[2,2,16,8192]{3,2,1,0:T(8,128)S(1)}, f32[2,2,16,8192]{3,2,1,0:T(8,128)}, u32[]{:S(2)}) copy-start(f32[2,2,16,8192]{3,2,1,0:T(8,128)} %filter_ref.1) | copy-start | bytes 6291460
  12.5 19.2 %collective-permute-start.11 = (f32[2,2,64,128]{3,2,1,0:T(8,128)S(1)}, f32[2,2,64,128]{3,2,1,0:T(8,128)S(1)}, u32[]{:S(2)}, u32[]{:S(2)}) collective-permute-start(f32[2,2,64,128]{3,2,1,0:T(8,128)S(1)} %get-tuple-element.44), channel_id=1, source_target_pairs={{0,4},{4,0},{8,12},{12,8},{16,20},{20,16},{24,28},{28,24},{1,5},{5... | collective-permute-start | bytes 393224 | tf_op jit(solution)/shard_map/ppermute | solution.py:309
  14.2 19.6 %collective-permute-start.12 = (f32[2,2,64,128]{3,2,1,0:T(8,128)S(1)}, f32[2,2,64,128]{3,2,1,0:T(8,128)S(1)}, u32[]{:S(2)}, u32[]{:S(2)}) collective-permute-start(f32[2,2,64,128]{3,2,1,0:T(8,128)S(1)} %get-tuple-element.45), channel_id=1, source_target_pairs={{0,16},{4,20},{8,24},{12,28},{16,0},{20,4},{24,8},{28,12},{1,17},{... | collective-permute-start | bytes 393224 | tf_op jit(solution)/shard_map/ppermute | solution.py:309
  14.5 13.9 %collective-permute-start.4 = (f32[128,128]{1,0:T(8,128)S(1)}, f32[128,128]{1,0:T(8,128)S(1)}, u32[]{:S(2)}, u32[]{:S(2)}) collective-permute-start(f32[128,128]{1,0:T(8,128)S(1)} %get-tuple-element.36), channel_id=1, source_target_pairs={{0,20},{4,16},{8,28},{12,24},{16,4},{20,0},{24,12},{28,8},{1,21},{... | collective-permute-start | bytes 196616 | tf_op jit(solution)/shard_map/ppermute | solution.py:309
  16.9 11.5 %collective-permute-start.5 = (f32[128,128]{1,0:T(8,128)S(1)}, f32[128,128]{1,0:T(8,128)S(1)}, u32[]{:S(2)}, u32[]{:S(2)}) collective-permute-start(f32[128,128]{1,0:T(8,128)S(1)} %get-tuple-element.37), channel_id=1, source_target_pairs={{0,24},{4,28},{8,16},{12,20},{16,8},{20,12},{24,0},{28,4},{1,25},{... | collective-permute-start | bytes 196616 | tf_op jit(solution)/shard_map/ppermute | solution.py:309
  18.4 12.4 %collective-permute-start.6 = (f32[128,128]{1,0:T(8,128)S(1)}, f32[128,128]{1,0:T(8,128)S(1)}, u32[]{:S(2)}, u32[]{:S(2)}) collective-permute-start(f32[128,128]{1,0:T(8,128)S(1)} %get-tuple-element.38), channel_id=1, source_target_pairs={{0,28},{4,24},{8,20},{12,16},{16,12},{20,8},{24,4},{28,0},{1,29},{... | collective-permute-start | bytes 196616 | tf_op jit(solution)/shard_map/ppermute | solution.py:309
  28.4 12.9 %collective-permute-start.7 = (f32[2,2,64,128]{3,2,1,0:T(8,128)S(1)}, f32[2,2,64,128]{3,2,1,0:T(8,128)S(1)}, u32[]{:S(2)}, u32[]{:S(2)}) collective-permute-start(f32[2,2,64,128]{3,2,1,0:T(8,128)S(1)} %get-tuple-element.39), channel_id=1, source_target_pairs={{0,8},{4,12},{8,0},{12,4},{16,24},{20,28},{24,16},{28,20},{1,9},{5... | collective-permute-start | bytes 393224 | tf_op jit(solution)/shard_map/ppermute | solution.py:309
  28.4 11.6 %collective-permute-start.13 = (f32[2,2,64,128]{3,2,1,0:T(8,128)S(1)}, f32[2,2,64,128]{3,2,1,0:T(8,128)S(1)}, u32[]{:S(2)}, u32[]{:S(2)}) collective-permute-start(f32[2,2,64,128]{3,2,1,0:T(8,128)S(1)} %get-tuple-element.46), channel_id=1, source_target_pairs={{0,20},{4,16},{8,28},{12,24},{16,4},{20,0},{24,12},{28,8},{1,21},{... | collective-permute-start | bytes 393224 | tf_op jit(solution)/shard_map/ppermute | solution.py:309
  30.9 10.5 %collective-permute-start.8 = (f32[2,2,64,128]{3,2,1,0:T(8,128)S(1)}, f32[2,2,64,128]{3,2,1,0:T(8,128)S(1)}, u32[]{:S(2)}, u32[]{:S(2)}) collective-permute-start(f32[2,2,64,128]{3,2,1,0:T(8,128)S(1)} %get-tuple-element.40), channel_id=1, source_target_pairs={{0,12},{4,8},{8,4},{12,0},{16,28},{20,24},{24,20},{28,16},{1,13},{... | collective-permute-start | bytes 393224 | tf_op jit(solution)/shard_map/ppermute | solution.py:309
  31.6 10.7 %collective-permute-start.9 = (f32[2,2,64,128]{3,2,1,0:T(8,128)S(1)}, f32[2,2,64,128]{3,2,1,0:T(8,128)S(1)}, u32[]{:S(2)}, u32[]{:S(2)}) collective-permute-start(f32[2,2,64,128]{3,2,1,0:T(8,128)S(1)} %get-tuple-element.41), channel_id=1, source_target_pairs={{0,24},{4,28},{8,16},{12,20},{16,8},{20,12},{24,0},{28,4},{1,25},{... | collective-permute-start | bytes 393224 | tf_op jit(solution)/shard_map/ppermute | solution.py:309
  33.8 10.7 %collective-permute-start.10 = (f32[2,2,64,128]{3,2,1,0:T(8,128)S(1)}, f32[2,2,64,128]{3,2,1,0:T(8,128)S(1)}, u32[]{:S(2)}, u32[]{:S(2)}) collective-permute-start(f32[2,2,64,128]{3,2,1,0:T(8,128)S(1)} %get-tuple-element.42), channel_id=1, source_target_pairs={{0,28},{4,24},{8,20},{12,16},{16,12},{20,8},{24,4},{28,0},{1,29},{... | collective-permute-start | bytes 393224 | tf_op jit(solution)/shard_map/ppermute | solution.py:309
  35.6 1.0 %copy-start.6 = (bf16[4,256,256]{2,1,0:T(8,128)(2,1)S(1)}, bf16[4,256,256]{2,1,0:T(8,128)(2,1)}, u32[]{:S(2)}) copy-start(bf16[4,256,256]{2,1,0:T(8,128)(2,1)} %constant.16.clone.refs_10_) | copy-start | bytes 1572868
  36.7 3.3 %copy-start.5 = (bf16[4,256,256]{2,1,0:T(8,128)(2,1)S(1)}, bf16[4,256,256]{2,1,0:T(8,128)(2,1)}, u32[]{:S(2)}) copy-start(bf16[4,256,256]{2,1,0:T(8,128)(2,1)} %constant.17.clone.refs_6_) | copy-start | bytes 1572868
  41.3 17.6 %copy-start.4 = (f32[16,8192]{1,0:T(8,128)S(1)}, f32[16,8192]{1,0:T(8,128)}, u32[]{:S(2)}) copy-start(f32[16,8192]{1,0:T(8,128)} %signal_ref.3) | copy-start | bytes 1572868
  41.3 17.6 %copy-start.7 = (f32[16,8192]{1,0:T(8,128)S(1)}, f32[16,8192]{1,0:T(8,128)}, u32[]{:S(2)}) copy-start(f32[16,8192]{1,0:T(8,128)} %gate_ref.1) | copy-start | bytes 1572868
  41.3 17.6 %copy-start.8 = (f32[16]{0:T(128)S(1)}, f32[16]{0:T(128)}, u32[]{:S(2)}) copy-start(f32[16]{0:T(128)} %skip_ref.1) | copy-start | bytes 196
  45.8 8.9 %collective-permute-start.14 = (f32[128,128]{1,0:T(8,128)S(1)}, f32[128,128]{1,0:T(8,128)S(1)}, u32[]{:S(2)}, u32[]{:S(2)}) collective-permute-start(f32[128,128]{1,0:T(8,128)S(1)} %get-tuple-element.48), channel_id=1, source_target_pairs={{0,4},{4,0},{8,12},{12,8},{16,20},{20,16},{24,28},{28,24},{1,5},{5... | collective-permute-start | bytes 196616 | tf_op jit(solution)/shard_map/ppermute | solution.py:309
  48.0 8.3 %collective-permute-start.15 = (f32[128,128]{1,0:T(8,128)S(1)}, f32[128,128]{1,0:T(8,128)S(1)}, u32[]{:S(2)}, u32[]{:S(2)}) collective-permute-start(f32[128,128]{1,0:T(8,128)S(1)} %get-tuple-element.49), channel_id=1, source_target_pairs={{0,8},{4,12},{8,0},{12,4},{16,24},{20,28},{24,16},{28,20},{1,9},{5... | collective-permute-start | bytes 196616 | tf_op jit(solution)/shard_map/ppermute | solution.py:309
  50.9 8.6 %collective-permute-start.16 = (f32[128,128]{1,0:T(8,128)S(1)}, f32[128,128]{1,0:T(8,128)S(1)}, u32[]{:S(2)}, u32[]{:S(2)}) collective-permute-start(f32[128,128]{1,0:T(8,128)S(1)} %get-tuple-element.50), channel_id=1, source_target_pairs={{0,12},{4,8},{8,4},{12,0},{16,28},{20,24},{24,20},{28,16},{1,13},{... | collective-permute-start | bytes 196616 | tf_op jit(solution)/shard_map/ppermute | solution.py:309
  51.2 8.8 %collective-permute-start.17 = (f32[128,128]{1,0:T(8,128)S(1)}, f32[128,128]{1,0:T(8,128)S(1)}, u32[]{:S(2)}, u32[]{:S(2)}) collective-permute-start(f32[128,128]{1,0:T(8,128)S(1)} %get-tuple-element.51), channel_id=1, source_target_pairs={{0,16},{4,20},{8,24},{12,28},{16,0},{20,4},{24,8},{28,12},{1,17},{... | collective-permute-start | bytes 196616 | tf_op jit(solution)/shard_map/ppermute | solution.py:309
  53.3 10.2 %collective-permute-start.18 = (f32[128,128]{1,0:T(8,128)S(1)}, f32[128,128]{1,0:T(8,128)S(1)}, u32[]{:S(2)}, u32[]{:S(2)}) collective-permute-start(f32[128,128]{1,0:T(8,128)S(1)} %get-tuple-element.52), channel_id=1, source_target_pairs={{0,20},{4,16},{8,28},{12,24},{16,4},{20,0},{24,12},{28,8},{1,21},{... | collective-permute-start | bytes 196616 | tf_op jit(solution)/shard_map/ppermute | solution.py:309
  54.8 8.7 %collective-permute-start.19 = (f32[128,128]{1,0:T(8,128)S(1)}, f32[128,128]{1,0:T(8,128)S(1)}, u32[]{:S(2)}, u32[]{:S(2)}) collective-permute-start(f32[128,128]{1,0:T(8,128)S(1)} %get-tuple-element.53), channel_id=1, source_target_pairs={{0,24},{4,28},{8,16},{12,20},{16,8},{20,12},{24,0},{28,4},{1,25},{... | collective-permute-start | bytes 196616 | tf_op jit(solution)/shard_map/ppermute | solution.py:309
  56.2 7.2 %collective-permute-start.20 = (f32[128,128]{1,0:T(8,128)S(1)}, f32[128,128]{1,0:T(8,128)S(1)}, u32[]{:S(2)}, u32[]{:S(2)}) collective-permute-start(f32[128,128]{1,0:T(8,128)S(1)} %get-tuple-element.54), channel_id=1, source_target_pairs={{0,28},{4,24},{8,20},{12,16},{16,12},{20,8},{24,4},{28,0},{1,29},{... | collective-permute-start | bytes 196616 | tf_op jit(solution)/shard_map/ppermute | solution.py:309
where the time goes:
time: 64.9 us; the launch traced here: 64.7 us
  starting transfers between devices  37.2 us (57%)
  waiting for transfers between devices  14.6 us (22%)
  Pallas kernels  8.96 us (14%)
  local copies, waits for them, and re-layouts  3.85 us (6%)
    ppermute x21, starting transfers between devices, exchange(): lax.ppermute(blocks[step], 'ctx', [(one, one ^ step) for one in range(par...  37.2 us
    ppermute x21, waiting for transfers between devices, exchange(): lax.ppermute(blocks[step], 'ctx', [(one, one ^ step) for one in range(par...  14.6 us
    pallas_call x7, Pallas kernels, call(): result = run(device, *operands)  8.96 us
    unnamed x18, local copies, waits for them, and re-layouts  3.85 us
  transfers between devices with their start and end apart: 21, of which 6 were waited for; matrix products, arithmetic and copies ran while one was open for 0% of the time, Pallas kernels for 9%

commit v1 on v0

--- a/solution.py
+++ b/solution.py
@@ -12,6 +12,7 @@
 
 LANES = 128
 HALF = LANES // 2
+FINE = 16
 
 
 def split_pair(values):
@@ -50,7 +51,6 @@
     freq_rows = 2 * parts
     period = freq_rows * blocks
     full_len = period * LANES
-    rows = np.arange(parts * blocks)
     index = np.zeros((parts, blocks), np.int64)
     for owner in range(parts):
         for place in range(blocks):
@@ -61,15 +61,26 @@
             else:
                 index[owner, place] = freq_rows * place + parts
     index = index.reshape(-1)
-    angle = 2 * np.pi * ((index[:, None] * rows[None, :]) % period) / period
-    wave_re, wave_im = np.cos(angle), -np.sin(angle)
-    wave_im[0] = np.where(rows % 2 == 0, 1.0, -1.0)
-    outer = np.stack([wave_re.reshape(-1, LANES, rows.size), wave_im.reshape(-1, LANES, rows.size)], axis=1)
-    outer = outer.reshape(-1, rows.size)
+
+    def wave(rows):
+        angle = 2 * np.pi * ((rows[:, None] * index[None, :]) % period) / period
+        return np.cos(angle), np.sin(angle)
+
+    def paired(re, im):
+        return np.stack([re.reshape(len(re), -1, LANES), im.reshape(len(im), -1, LANES)], axis=2).reshape(len(re), -1)
+
+    coarse_rows, fine_rows = np.arange(0, parts * blocks, FINE), np.arange(FINE)
+    (coarse_cos, coarse_sin), (fine_cos, fine_sin) = wave(coarse_rows), wave(fine_rows)
+    coarse = np.stack([paired(coarse_cos, -coarse_sin), paired(-coarse_sin, -coarse_cos)])
+    fine = np.stack([paired(fine_cos, fine_cos), paired(fine_sin, fine_sin)])
+    coarse[0, :, LANES], coarse[1, :, LANES] = 1.0, 0.0
+    fine[0, :, LANES] = np.where(fine_rows % 2 == 0, 1.0, -1.0)
     lane = np.arange(LANES)
-    turn = 2 * np.pi * ((index[:, None] * lane[None, :]) % full_len) / full_len
-    twist = np.stack([np.cos(turn), np.sin(turn)])
-    twist[0, 0], twist[1, 0] = 1.0, 0.0
+
+    def turn(rows):
+        angle = 2 * np.pi * ((rows[:, None] * lane[None, :]) % full_len) / full_len
+        return np.stack([np.cos(angle), np.sin(angle)])
+
     freq = 2 * (lane % HALF) + lane // HALF
     theta = 2 * np.pi * ((lane[:, None] * freq[None, :]) % LANES) / LANES
     cos, sin = np.cos(theta), np.sin(theta)
@@ -89,11 +100,32 @@
     back_im = np.concatenate([(zero_im * weight).T, mid_im.T], axis=1)
     edge_back = np.concatenate([back_re, back_im], axis=0) / full_len
     return {
-        "outer": split_table(outer.T),
-        "twist": twist.astype(np.float32),
+        "coarse": coarse.astype(np.float32),
+        "fine": fine.astype(np.float32),
+        "place": turn(freq_rows * np.arange(blocks)).astype(np.float32),
+        "owner": turn(np.arange(parts + 1)).astype(np.float32),
         "there": np.concatenate([split_table(inner), split_table(edge)]),
         "back": np.concatenate([split_table(inner_back), split_table(edge_back)]),
     }
+
+
+def table_kernel(coarse_ref, fine_ref, place_ref, owner_ref, outer_ref, twist_ref):
+    for index in range(coarse_ref.shape[1]):
+        rows = slice(index * FINE, (index + 1) * FINE)
+        values = coarse_ref[0, index : index + 1] * fine_ref[0] + coarse_ref[1, index : index + 1] * fine_ref[1]
+        for level, piece in enumerate(split_pair(values)):
+            outer_ref[level, rows] = piece
+    blocks, parts = place_ref.shape[1], owner_ref.shape[1] - 1
+    cos, sin = place_ref[0], place_ref[1]
+    for owner in range(1, parts + 1):
+        step_cos, step_sin = owner_ref[0, owner : owner + 1], owner_ref[1, owner : owner + 1]
+        both = (cos * step_cos - sin * step_sin, sin * step_cos + cos * step_sin)
+        for part, values in enumerate(both):
+            if owner < parts:
+                twist_ref[part, owner * blocks : (owner + 1) * blocks] = values
+            else:
+                twist_ref[part, blocks // 2 : blocks] = values[blocks // 2 :]
+                twist_ref[part, : blocks // 2] = place_ref[part, : blocks // 2]
 
 
 def spread_kernel(device_ref, signal_ref, *refs):
@@ -285,19 +317,20 @@
         out_ref[:, where] = scale_ref[:, where] * conv + base_ref[:, where]
 
 
-def call(kernel, shapes, device, *operands, scratch, limit):
+def call(kernel, shapes, *operands, scratch, limit, scalars=1):
     one = not isinstance(shapes, list)
     shapes = [shapes] if one else shapes
-    vmem = pl.BlockSpec(memory_space=pltpu.VMEM)
+    shapes = [shape if hasattr(shape, "dtype") else jax.ShapeDtypeStruct(shape, jnp.float32) for shape in shapes]
+    vmem, smem = pl.BlockSpec(memory_space=pltpu.VMEM), pl.BlockSpec(memory_space=pltpu.SMEM)
     run = pl.pallas_call(
         kernel,
-        out_shape=[jax.ShapeDtypeStruct(shape, jnp.float32) for shape in shapes],
-        in_specs=[pl.BlockSpec(memory_space=pltpu.SMEM)] + [vmem] * len(operands),
+        out_shape=shapes,
+        in_specs=[smem] * scalars + [vmem] * (len(operands) - scalars),
         out_specs=[vmem] * len(shapes),
         scratch_shapes=scratch,
         compiler_params=pltpu.CompilerParams(vmem_limit_bytes=limit << 20),
     )
-    result = run(device, *operands)
+    result = run(*operands)
     return result[0] if one else result
 
 
@@ -331,18 +364,29 @@
         limit=10,
     )
     filt = exchange(folded)
+    outer, twist = call(
+        table_kernel,
+        [jax.ShapeDtypeStruct((2, slots, 2 * slots), jnp.bfloat16), (2, slots, LANES)],
+        table["coarse"],
+        table["fine"],
+        table["place"],
+        table["owner"],
+        scratch=[],
+        limit=8,
+        scalars=0,
+    )
     spectrum = call(
         functools.partial(forward_kernel, own=own),
         (own, 2, slots, LANES),
         device,
         *columns,
-        table["outer"],
-        table["twist"],
+        outer,
+        twist,
         table["there"],
         scratch=[pltpu.VMEM((slots, own * LANES), jnp.float32)],
         limit=12,
     )
-    back_tables = (table["outer"], table["twist"], table["back"])
+    back_tables = (outer, twist, table["back"])
     early, late = split_steps(parts)
     product = pltpu.VMEM((2, own, slots // 2, 2 * LANES), jnp.bfloat16)
     partial = call(

time: 64.9 us -> 63.9 us (0.985)
  waiting for transfers between devices: 14.6 us -> 12.5 us
  starting transfers between devices: 37.2 us -> 38.8 us
  local copies, waits for them, and re-layouts: 3.85 us -> 2.68 us
    ppermute x21, waiting for transfers between devices: 14.6 us -> 12.5 us  [exchange(): lax.ppermute(blocks[step], 'ctx', [(one, one ^ step) for one in range(par...]
    ppermute x21, starting transfers between devices: 37.2 us -> 38.8 us  [exchange(): lax.ppermute(blocks[step], 'ctx', [(one, one ^ step) for one in range(par...]
    unnamed x18 -> x22, local copies, waits for them, and re-layouts: 3.85 us -> 2.68 us
    pallas_call x7 -> x8, Pallas kernels: 8.96 us -> 9.57 us  [call(): result = run(*operands)]
  transfers between devices with their start and end apart: 21 -> 21, of which waited for: 6 -> 4; matrix products, arithmetic and copies ran while one was open for 0% -> 0% of each run, Pallas kernels for 9% -> 10%
where the time goes in v1:
time: 63.9 us; the launch traced here: 63.7 us
  starting transfers between devices  38.8 us (61%)
  waiting for transfers between devices  12.5 us (20%)
  Pallas kernels  9.57 us (15%)
  local copies, waits for them, and re-layouts  2.68 us (4%)
    ppermute x21, starting transfers between devices, exchange(): lax.ppermute(blocks[step], 'ctx', [(one, one ^ step) for one in range(par...  38.8 us
    ppermute x21, waiting for transfers between devices, exchange(): lax.ppermute(blocks[step], 'ctx', [(one, one ^ step) for one in range(par...  12.5 us
    pallas_call x8, Pallas kernels, call(): result = run(*operands)  9.57 us
    unnamed x22, local copies, waits for them, and re-layouts  2.68 us
  transfers between devices with their start and end apart: 21, of which 4 were waited for; matrix products, arithmetic and copies ran while one was open for 0% of the time, Pallas kernels for 10%

profile of v1, /device:TPU:0, one launch (start us, length us, event | category | flops | bytes accessed | tf_op | source)
XLA Modules:
  0.0 63.7 jit_solution(11721974938376982499)
XLA Ops:
  0.0 1.0 %copy-done.1 = f32[16,8192]{1,0:T(8,128)S(1)} copy-done((f32[16,8192]{1,0:T(8,128)S(1)}, f32[16,8192]{1,0:T(8,128)}, u32[]{:S(2)}) %copy-start.1) | copy-done | bytes 524312
  1.0 0.5 shard_map.100
  1.5 3.0 %collective-permute-start = (f32[128,128]{1,0:T(8,128)S(1)}, f32[128,128]{1,0:T(8,128)S(1)}, u32[]{:S(2)}, u32[]{:S(2)}) collective-permute-start(f32[128,128]{1,0:T(8,128)S(1)} %get-tuple-element.34), channel_id=1, source_target_pairs={{0,4},{4,0},{8,12},{12,8},{16,20},{20,16},{24,28},{28,24},{1,5},{5... | collective-permute-start | bytes 196616 | tf_op jit(solution)/shard_map/ppermute | solution.py:342
  4.6 1.6 %collective-permute-start.1 = (f32[128,128]{1,0:T(8,128)S(1)}, f32[128,128]{1,0:T(8,128)S(1)}, u32[]{:S(2)}, u32[]{:S(2)}) collective-permute-start(f32[128,128]{1,0:T(8,128)S(1)} %get-tuple-element.35), channel_id=1, source_target_pairs={{0,8},{4,12},{8,0},{12,4},{16,24},{20,28},{24,16},{28,20},{1,9},{5... | collective-permute-start | bytes 196616 | tf_op jit(solution)/shard_map/ppermute | solution.py:342
  6.1 3.0 %collective-permute-start.3 = (f32[128,128]{1,0:T(8,128)S(1)}, f32[128,128]{1,0:T(8,128)S(1)}, u32[]{:S(2)}, u32[]{:S(2)}) collective-permute-start(f32[128,128]{1,0:T(8,128)S(1)} %get-tuple-element.37), channel_id=1, source_target_pairs={{0,16},{4,20},{8,24},{12,28},{16,0},{20,4},{24,8},{28,12},{1,17},{... | collective-permute-start | bytes 196616 | tf_op jit(solution)/shard_map/ppermute | solution.py:342
  9.2 1.6 %copy-done = f32[2,2,16,8192]{3,2,1,0:T(8,128)S(1)} copy-done((f32[2,2,16,8192]{3,2,1,0:T(8,128)S(1)}, f32[2,2,16,8192]{3,2,1,0:T(8,128)}, u32[]{:S(2)}) %copy-start) | copy-done | bytes 2097176
  10.8 1.6 %shard_map.103 = (f32[2,2,64,128]{3,2,1,0:T(8,128)S(1)}, f32[2,2,64,128]{3,2,1,0:T(8,128)S(1)}, f32[2,2,64,128]{3,2,1,0:T(8,128)S(1)}, f32[2,2,64,128]{3,2,1,0:T...) custom-call(s32[1]{0:T(128)} %bitcast.device_ref, ...), custom_call_target="tpu_custom_call" | custom-call | tf_op jit(solution)/shard_map/pallas_call | solution.py:333
  12.3 1.7 %collective-permute-start.11 = (f32[2,2,64,128]{3,2,1,0:T(8,128)S(1)}, f32[2,2,64,128]{3,2,1,0:T(8,128)S(1)}, u32[]{:S(2)}, u32[]{:S(2)}) collective-permute-start(f32[2,2,64,128]{3,2,1,0:T(8,128)S(1)} %get-tuple-element.48), channel_id=1, source_target_pairs={{0,4},{4,0},{8,12},{12,8},{16,20},{20,16},{24,28},{28,24},{1,5},{5... | collective-permute-start | bytes 393224 | tf_op jit(solution)/shard_map/ppermute | solution.py:342
  14.1 0.3 collective-permute-start.12
  14.4 2.4 %collective-permute-start.4 = (f32[128,128]{1,0:T(8,128)S(1)}, f32[128,128]{1,0:T(8,128)S(1)}, u32[]{:S(2)}, u32[]{:S(2)}) collective-permute-start(f32[128,128]{1,0:T(8,128)S(1)} %get-tuple-element.38), channel_id=1, source_target_pairs={{0,20},{4,16},{8,28},{12,24},{16,4},{20,0},{24,12},{28,8},{1,21},{... | collective-permute-start | bytes 196616 | tf_op jit(solution)/shard_map/ppermute | solution.py:342
  16.8 1.5 %collective-permute-start.5 = (f32[128,128]{1,0:T(8,128)S(1)}, f32[128,128]{1,0:T(8,128)S(1)}, u32[]{:S(2)}, u32[]{:S(2)}) collective-permute-start(f32[128,128]{1,0:T(8,128)S(1)} %get-tuple-element.39), channel_id=1, source_target_pairs={{0,24},{4,28},{8,16},{12,20},{16,8},{20,12},{24,0},{28,4},{1,25},{... | collective-permute-start | bytes 196616 | tf_op jit(solution)/shard_map/ppermute | solution.py:342
  18.3 3.4 %collective-permute-start.6 = (f32[128,128]{1,0:T(8,128)S(1)}, f32[128,128]{1,0:T(8,128)S(1)}, u32[]{:S(2)}, u32[]{:S(2)}) collective-permute-start(f32[128,128]{1,0:T(8,128)S(1)} %get-tuple-element.40), channel_id=1, source_target_pairs={{0,28},{4,24},{8,20},{12,16},{16,12},{20,8},{24,4},{28,0},{1,29},{... | collective-permute-start | bytes 196616 | tf_op jit(solution)/shard_map/ppermute | solution.py:342
  21.7 6.6 %collective-permute-done.4.refs_5_ = f32[128,128]{1,0:T(8,128)S(1)} collective-permute-done((f32[128,128]{1,0:T(8,128)S(1)}, f32[128,128]{1,0:T(8,128)S(1)}, u32[]{:S(2)}, u32[]{:S(2)}) %collective-permute-start.4) | collective-permute-done | bytes 65568 | tf_op jit(solution)/shard_map/ppermute | solution.py:342
  28.3 1.9 %collective-permute-start.10 = (f32[2,2,64,128]{3,2,1,0:T(8,128)S(1)}, f32[2,2,64,128]{3,2,1,0:T(8,128)S(1)}, u32[]{:S(2)}, u32[]{:S(2)}) collective-permute-start(f32[2,2,64,128]{3,2,1,0:T(8,128)S(1)} %get-tuple-element.46), channel_id=1, source_target_pairs={{0,28},{4,24},{8,20},{12,16},{16,12},{20,8},{24,4},{28,0},{1,29},{... | collective-permute-start | bytes 393224 | tf_op jit(solution)/shard_map/ppermute | solution.py:342
  30.2 6.4 %collective-permute-start.7 = (f32[2,2,64,128]{3,2,1,0:T(8,128)S(1)}, f32[2,2,64,128]{3,2,1,0:T(8,128)S(1)}, u32[]{:S(2)}, u32[]{:S(2)}) collective-permute-start(f32[2,2,64,128]{3,2,1,0:T(8,128)S(1)} %get-tuple-element.43), channel_id=1, source_target_pairs={{0,8},{4,12},{8,0},{12,4},{16,24},{20,28},{24,16},{28,20},{1,9},{5... | collective-permute-start | bytes 393224 | tf_op jit(solution)/shard_map/ppermute | solution.py:342
  36.8 1.6 %collective-permute-start.9 = (f32[2,2,64,128]{3,2,1,0:T(8,128)S(1)}, f32[2,2,64,128]{3,2,1,0:T(8,128)S(1)}, u32[]{:S(2)}, u32[]{:S(2)}) collective-permute-start(f32[2,2,64,128]{3,2,1,0:T(8,128)S(1)} %get-tuple-element.45), channel_id=1, source_target_pairs={{0,24},{4,28},{8,16},{12,20},{16,8},{20,12},{24,0},{28,4},{1,25},{... | collective-permute-start | bytes 393224 | tf_op jit(solution)/shard_map/ppermute | solution.py:342
  38.4 0.6 shard_map.101
  39.0 2.5 %shard_map.102.spectrum_ref = f32[2,2,512,128]{3,2,1,0:T(8,128)S(1)} custom-call(s32[1]{0:T(128)} %bitcast.device_ref, f32[128,128]{1,0:T(8,128)S(1)} %get-tuple-element.33.refs_0_, f32[128,128]{1,0:T(8,128)S(1)} %collective-permute-done.refs_1_, f32[128,128]{1,0:T(8,128)S(1)} %collective-permute-done.1.refs_2_, ...), custom_call_target="tpu_custom_call" | custom-call | tf_op jit(solution)/shard_map/pallas_call | solution.py:333
  41.6 1.3 %shard_map.104.refs_7_ = f32[512,256]{1,0:T(8,128)S(1)} custom-call(s32[1]{0:T(128)} %bitcast.device_ref, f32[2,2,512,128]{3,2,1,0:T(8,128)S(1)} %shard_map.102.spectrum_ref, f32[2,2,64,128]{3,2,1,0:T(8,128)S(1)} %get-tuple-element.47.refs_0_, f32[2,2,64,128]{3,2,1,0:T(8,128)S(1)} %collective-permute-done.11.refs_1_, ...), custom_call_target="tpu_custom_call" | custom-call | tf_op jit(solution)/shard_map/pallas_call | solution.py:333
  42.9 1.9 %collective-permute-done.8.refs_1_ = f32[2,2,64,128]{3,2,1,0:T(8,128)S(1)} collective-permute-done((f32[2,2,64,128]{3,2,1,0:T(8,128)S(1)}, f32[2,2,64,128]{3,2,1,0:T(8,128)S(1)}, u32[]{:S(2)}, u32[]{:S(2)}) %collective-permute-start.8) | collective-permute-done | bytes 131104 | tf_op jit(solution)/shard_map/ppermute | solution.py:342
  44.9 1.3 %shard_map.105 = (f32[128,128]{1,0:T(8,128)S(1)}, f32[128,128]{1,0:T(8,128)S(1)}, f32[128,128]{1,0:T(8,128)S(1)}, f32[128,128]{1,0:T(8,128)S(1)}, f32[128,128]{1...) custom-call(s32[1]{0:T(128)} %bitcast.device_ref, ...), custom_call_target="tpu_custom_call" | custom-call | tf_op jit(solution)/shard_map/pallas_call | solution.py:333
  46.2 1.4 %collective-permute-start.14 = (f32[128,128]{1,0:T(8,128)S(1)}, f32[128,128]{1,0:T(8,128)S(1)}, u32[]{:S(2)}, u32[]{:S(2)}) collective-permute-start(f32[128,128]{1,0:T(8,128)S(1)} %get-tuple-element.52), channel_id=1, source_target_pairs={{0,4},{4,0},{8,12},{12,8},{16,20},{20,16},{24,28},{28,24},{1,5},{5... | collective-permute-start | bytes 196616 | tf_op jit(solution)/shard_map/ppermute | solution.py:342
  47.6 1.6 %collective-permute-start.15 = (f32[128,128]{1,0:T(8,128)S(1)}, f32[128,128]{1,0:T(8,128)S(1)}, u32[]{:S(2)}, u32[]{:S(2)}) collective-permute-start(f32[128,128]{1,0:T(8,128)S(1)} %get-tuple-element.53), channel_id=1, source_target_pairs={{0,8},{4,12},{8,0},{12,4},{16,24},{20,28},{24,16},{28,20},{1,9},{5... | collective-permute-start | bytes 196616 | tf_op jit(solution)/shard_map/ppermute | solution.py:342
  49.2 1.1 %collective-permute-start.16 = (f32[128,128]{1,0:T(8,128)S(1)}, f32[128,128]{1,0:T(8,128)S(1)}, u32[]{:S(2)}, u32[]{:S(2)}) collective-permute-start(f32[128,128]{1,0:T(8,128)S(1)} %get-tuple-element.54), channel_id=1, source_target_pairs={{0,12},{4,8},{8,4},{12,0},{16,28},{20,24},{24,20},{28,16},{1,13},{... | collective-permute-start | bytes 196616 | tf_op jit(solution)/shard_map/ppermute | solution.py:342
  50.3 1.8 %collective-permute-start.17 = (f32[128,128]{1,0:T(8,128)S(1)}, f32[128,128]{1,0:T(8,128)S(1)}, u32[]{:S(2)}, u32[]{:S(2)}) collective-permute-start(f32[128,128]{1,0:T(8,128)S(1)} %get-tuple-element.55), channel_id=1, source_target_pairs={{0,16},{4,20},{8,24},{12,28},{16,0},{20,4},{24,8},{28,12},{1,17},{... | collective-permute-start | bytes 196616 | tf_op jit(solution)/shard_map/ppermute | solution.py:342
  52.1 1.4 %collective-permute-start.18 = (f32[128,128]{1,0:T(8,128)S(1)}, f32[128,128]{1,0:T(8,128)S(1)}, u32[]{:S(2)}, u32[]{:S(2)}) collective-permute-start(f32[128,128]{1,0:T(8,128)S(1)} %get-tuple-element.56), channel_id=1, source_target_pairs={{0,20},{4,16},{8,28},{12,24},{16,4},{20,0},{24,12},{28,8},{1,21},{... | collective-permute-start | bytes 196616 | tf_op jit(solution)/shard_map/ppermute | solution.py:342
  53.5 1.8 %collective-permute-start.19 = (f32[128,128]{1,0:T(8,128)S(1)}, f32[128,128]{1,0:T(8,128)S(1)}, u32[]{:S(2)}, u32[]{:S(2)}) collective-permute-start(f32[128,128]{1,0:T(8,128)S(1)} %get-tuple-element.57), channel_id=1, source_target_pairs={{0,24},{4,28},{8,16},{12,20},{16,8},{20,12},{24,0},{28,4},{1,25},{... | collective-permute-start | bytes 196616 | tf_op jit(solution)/shard_map/ppermute | solution.py:342
  55.3 2.6 %collective-permute-start.20 = (f32[128,128]{1,0:T(8,128)S(1)}, f32[128,128]{1,0:T(8,128)S(1)}, u32[]{:S(2)}, u32[]{:S(2)}) collective-permute-start(f32[128,128]{1,0:T(8,128)S(1)} %get-tuple-element.58), channel_id=1, source_target_pairs={{0,28},{4,24},{8,20},{12,16},{16,12},{20,8},{24,4},{28,0},{1,29},{... | collective-permute-start | bytes 196616 | tf_op jit(solution)/shard_map/ppermute | solution.py:342
  58.0 0.6 shard_map.106
  58.6 1.6 %collective-permute-done.17.refs_4_ = f32[128,128]{1,0:T(8,128)S(1)} collective-permute-done((f32[128,128]{1,0:T(8,128)S(1)}, f32[128,128]{1,0:T(8,128)S(1)}, u32[]{:S(2)}, u32[]{:S(2)}) %collective-permute-start.17) | collective-permute-done | bytes 65568 | tf_op jit(solution)/shard_map/ppermute | solution.py:342
  60.2 2.3 %collective-permute-done.18.refs_5_ = f32[128,128]{1,0:T(8,128)S(1)} collective-permute-done((f32[128,128]{1,0:T(8,128)S(1)}, f32[128,128]{1,0:T(8,128)S(1)}, u32[]{:S(2)}, u32[]{:S(2)}) %collective-permute-start.18) | collective-permute-done | bytes 65568 | tf_op jit(solution)/shard_map/ppermute | solution.py:342
  62.5 1.2 %shard_map.107 = f32[16,8192]{1,0:T(8,128)} custom-call(s32[1]{0:T(128)} %bitcast.device_ref, f32[128,128]{1,0:T(8,128)S(1)} %get-tuple-element.51.refs_0_, f32[128,128]{1,0:T(8,128)S(1)} %collective-permute-done.14.refs_1_, f32[128,128]{1,0:T(8,128)S(1)} %collective-permute-done.15.refs_2_, f32[128,128]{1,0:T(8,128)S(1)} %collective-permute-done.16.refs_3_, ...), custom_call_target="tpu_custom_call" | custom-call | tf_op jit(solution)/shard_map/pallas_call | solution.py:333
  (40 shorter events, 0.3 us)
Async XLA Ops:
  0.0 1.0 %copy-start.1 = (f32[16,8192]{1,0:T(8,128)S(1)}, f32[16,8192]{1,0:T(8,128)}, u32[]{:S(2)}) copy-start(f32[16,8192]{1,0:T(8,128)} %signal_ref.3) | copy-start | bytes 1572868
  1.0 38.0 %copy-start.4 = (bf16[4,256,256]{2,1,0:T(8,128)(2,1)S(1)}, bf16[4,256,256]{2,1,0:T(8,128)(2,1)}, u32[]{:S(2)}) copy-start(bf16[4,256,256]{2,1,0:T(8,128)(2,1)} %constant.22.clone.refs_10_) | copy-start | bytes 1572868
  1.5 12.5 %collective-permute-start = (f32[128,128]{1,0:T(8,128)S(1)}, f32[128,128]{1,0:T(8,128)S(1)}, u32[]{:S(2)}, u32[]{:S(2)}) collective-permute-start(f32[128,128]{1,0:T(8,128)S(1)} %get-tuple-element.34), channel_id=1, source_target_pairs={{0,4},{4,0},{8,12},{12,8},{16,20},{20,16},{24,28},{28,24},{1,5},{5... | collective-permute-start | bytes 196616 | tf_op jit(solution)/shard_map/ppermute | solution.py:342
  4.6 9.8 %collective-permute-start.1 = (f32[128,128]{1,0:T(8,128)S(1)}, f32[128,128]{1,0:T(8,128)S(1)}, u32[]{:S(2)}, u32[]{:S(2)}) collective-permute-start(f32[128,128]{1,0:T(8,128)S(1)} %get-tuple-element.35), channel_id=1, source_target_pairs={{0,8},{4,12},{8,0},{12,4},{16,24},{20,28},{24,16},{28,20},{1,9},{5... | collective-permute-start | bytes 196616 | tf_op jit(solution)/shard_map/ppermute | solution.py:342
  6.1 10.7 %collective-permute-start.2 = (f32[128,128]{1,0:T(8,128)S(1)}, f32[128,128]{1,0:T(8,128)S(1)}, u32[]{:S(2)}, u32[]{:S(2)}) collective-permute-start(f32[128,128]{1,0:T(8,128)S(1)} %get-tuple-element.36), channel_id=1, source_target_pairs={{0,12},{4,8},{8,4},{12,0},{16,28},{20,24},{24,20},{28,16},{1,13},{... | collective-permute-start | bytes 196616 | tf_op jit(solution)/shard_map/ppermute | solution.py:342
  6.1 12.2 %collective-permute-start.3 = (f32[128,128]{1,0:T(8,128)S(1)}, f32[128,128]{1,0:T(8,128)S(1)}, u32[]{:S(2)}, u32[]{:S(2)}) collective-permute-start(f32[128,128]{1,0:T(8,128)S(1)} %get-tuple-element.37), channel_id=1, source_target_pairs={{0,16},{4,20},{8,24},{12,28},{16,0},{20,4},{24,8},{28,12},{1,17},{... | collective-permute-start | bytes 196616 | tf_op jit(solution)/shard_map/ppermute | solution.py:342
  9.2 1.6 %copy-start = (f32[2,2,16,8192]{3,2,1,0:T(8,128)S(1)}, f32[2,2,16,8192]{3,2,1,0:T(8,128)}, u32[]{:S(2)}) copy-start(f32[2,2,16,8192]{3,2,1,0:T(8,128)} %filter_ref.1) | copy-start | bytes 6291460
  10.7 27.7 %copy-start.6 = (f32[2,32,1024]{2,1,0:T(8,128)S(1)}, f32[2,32,1024]{2,1,0:T(8,128)}, u32[]{:S(2)}) copy-start(f32[2,32,1024]{2,1,0:T(8,128)} %constant.18.clone.coarse_ref) | copy-start | bytes 786436
  10.7 27.7 %copy-start.7 = (f32[2,16,1024]{2,1,0:T(8,128)S(1)}, f32[2,16,1024]{2,1,0:T(8,128)}, u32[]{:S(2)}) copy-start(f32[2,16,1024]{2,1,0:T(8,128)} %constant.19.clone.fine_ref) | copy-start | bytes 393220
  10.8 27.7 %copy-start.8 = (f32[2,64,128]{2,1,0:T(8,128)S(1)}, f32[2,64,128]{2,1,0:T(8,128)}, u32[]{:S(2)}) copy-start(f32[2,64,128]{2,1,0:T(8,128)} %constant.20.clone.place_ref) | copy-start | bytes 196612
  10.8 27.7 %copy-start.9 = (f32[2,9,128]{2,1,0:T(8,128)S(1)}, f32[2,9,128]{2,1,0:T(8,128)}, u32[]{:S(2)}) copy-start(f32[2,9,128]{2,1,0:T(8,128)} %constant.21.clone.owner_ref) | copy-start | bytes 27652
  12.3 24.2 %collective-permute-start.11 = (f32[2,2,64,128]{3,2,1,0:T(8,128)S(1)}, f32[2,2,64,128]{3,2,1,0:T(8,128)S(1)}, u32[]{:S(2)}, u32[]{:S(2)}) collective-permute-start(f32[2,2,64,128]{3,2,1,0:T(8,128)S(1)} %get-tuple-element.48), channel_id=1, source_target_pairs={{0,4},{4,0},{8,12},{12,8},{16,20},{20,16},{24,28},{28,24},{1,5},{5... | collective-permute-start | bytes 393224 | tf_op jit(solution)/shard_map/ppermute | solution.py:342
  14.1 22.8 %collective-permute-start.12 = (f32[2,2,64,128]{3,2,1,0:T(8,128)S(1)}, f32[2,2,64,128]{3,2,1,0:T(8,128)S(1)}, u32[]{:S(2)}, u32[]{:S(2)}) collective-permute-start(f32[2,2,64,128]{3,2,1,0:T(8,128)S(1)} %get-tuple-element.49), channel_id=1, source_target_pairs={{0,16},{4,20},{8,24},{12,28},{16,0},{20,4},{24,8},{28,12},{1,17},{... | collective-permute-start | bytes 393224 | tf_op jit(solution)/shard_map/ppermute | solution.py:342
  14.4 13.9 %collective-permute-start.4 = (f32[128,128]{1,0:T(8,128)S(1)}, f32[128,128]{1,0:T(8,128)S(1)}, u32[]{:S(2)}, u32[]{:S(2)}) collective-permute-start(f32[128,128]{1,0:T(8,128)S(1)} %get-tuple-element.38), channel_id=1, source_target_pairs={{0,20},{4,16},{8,28},{12,24},{16,4},{20,0},{24,12},{28,8},{1,21},{... | collective-permute-start | bytes 196616 | tf_op jit(solution)/shard_map/ppermute | solution.py:342
  16.8 11.5 %collective-permute-start.5 = (f32[128,128]{1,0:T(8,128)S(1)}, f32[128,128]{1,0:T(8,128)S(1)}, u32[]{:S(2)}, u32[]{:S(2)}) collective-permute-start(f32[128,128]{1,0:T(8,128)S(1)} %get-tuple-element.39), channel_id=1, source_target_pairs={{0,24},{4,28},{8,16},{12,20},{16,8},{20,12},{24,0},{28,4},{1,25},{... | collective-permute-start | bytes 196616 | tf_op jit(solution)/shard_map/ppermute | solution.py:342
  18.3 11.9 %collective-permute-start.6 = (f32[128,128]{1,0:T(8,128)S(1)}, f32[128,128]{1,0:T(8,128)S(1)}, u32[]{:S(2)}, u32[]{:S(2)}) collective-permute-start(f32[128,128]{1,0:T(8,128)S(1)} %get-tuple-element.40), channel_id=1, source_target_pairs={{0,28},{4,24},{8,20},{12,16},{16,12},{20,8},{24,4},{28,0},{1,29},{... | collective-permute-start | bytes 196616 | tf_op jit(solution)/shard_map/ppermute | solution.py:342
  28.3 13.3 %collective-permute-start.13 = (f32[2,2,64,128]{3,2,1,0:T(8,128)S(1)}, f32[2,2,64,128]{3,2,1,0:T(8,128)S(1)}, u32[]{:S(2)}, u32[]{:S(2)}) collective-permute-start(f32[2,2,64,128]{3,2,1,0:T(8,128)S(1)} %get-tuple-element.50), channel_id=1, source_target_pairs={{0,20},{4,16},{8,28},{12,24},{16,4},{20,0},{24,12},{28,8},{1,21},{... | collective-permute-start | bytes 393224 | tf_op jit(solution)/shard_map/ppermute | solution.py:342
  28.3 14.6 %collective-permute-start.10 = (f32[2,2,64,128]{3,2,1,0:T(8,128)S(1)}, f32[2,2,64,128]{3,2,1,0:T(8,128)S(1)}, u32[]{:S(2)}, u32[]{:S(2)}) collective-permute-start(f32[2,2,64,128]{3,2,1,0:T(8,128)S(1)} %get-tuple-element.46), channel_id=1, source_target_pairs={{0,28},{4,24},{8,20},{12,16},{16,12},{20,8},{24,4},{28,0},{1,29},{... | collective-permute-start | bytes 393224 | tf_op jit(solution)/shard_map/ppermute | solution.py:342
  30.2 12.7 %collective-permute-start.7 = (f32[2,2,64,128]{3,2,1,0:T(8,128)S(1)}, f32[2,2,64,128]{3,2,1,0:T(8,128)S(1)}, u32[]{:S(2)}, u32[]{:S(2)}) collective-permute-start(f32[2,2,64,128]{3,2,1,0:T(8,128)S(1)} %get-tuple-element.43), channel_id=1, source_target_pairs={{0,8},{4,12},{8,0},{12,4},{16,24},{20,28},{24,16},{28,20},{1,9},{5... | collective-permute-start | bytes 393224 | tf_op jit(solution)/shard_map/ppermute | solution.py:342
  36.6 8.3 %collective-permute-start.8 = (f32[2,2,64,128]{3,2,1,0:T(8,128)S(1)}, f32[2,2,64,128]{3,2,1,0:T(8,128)S(1)}, u32[]{:S(2)}, u32[]{:S(2)}) collective-permute-start(f32[2,2,64,128]{3,2,1,0:T(8,128)S(1)} %get-tuple-element.44), channel_id=1, source_target_pairs={{0,12},{4,8},{8,4},{12,0},{16,28},{20,24},{24,20},{28,16},{1,13},{... | collective-permute-start | bytes 393224 | tf_op jit(solution)/shard_map/ppermute | solution.py:342
  36.8 8.0 %collective-permute-start.9 = (f32[2,2,64,128]{3,2,1,0:T(8,128)S(1)}, f32[2,2,64,128]{3,2,1,0:T(8,128)S(1)}, u32[]{:S(2)}, u32[]{:S(2)}) collective-permute-start(f32[2,2,64,128]{3,2,1,0:T(8,128)S(1)} %get-tuple-element.45), channel_id=1, source_target_pairs={{0,24},{4,28},{8,16},{12,20},{16,8},{20,12},{24,0},{28,4},{1,25},{... | collective-permute-start | bytes 393224 | tf_op jit(solution)/shard_map/ppermute | solution.py:342
  39.0 2.6 %copy-start.3 = (bf16[4,256,256]{2,1,0:T(8,128)(2,1)S(1)}, bf16[4,256,256]{2,1,0:T(8,128)(2,1)}, u32[]{:S(2)}) copy-start(bf16[4,256,256]{2,1,0:T(8,128)(2,1)} %constant.23.clone.refs_6_) | copy-start | bytes 1572868
  42.9 15.1 %copy-start.2 = (f32[16,8192]{1,0:T(8,128)S(1)}, f32[16,8192]{1,0:T(8,128)}, u32[]{:S(2)}) copy-start(f32[16,8192]{1,0:T(8,128)} %signal_ref.3) | copy-start | bytes 1572868
  42.9 15.1 %copy-start.5 = (f32[16,8192]{1,0:T(8,128)S(1)}, f32[16,8192]{1,0:T(8,128)}, u32[]{:S(2)}) copy-start(f32[16,8192]{1,0:T(8,128)} %gate_ref.1) | copy-start | bytes 1572868
  42.9 15.1 %copy-start.10 = (f32[16]{0:T(128)S(1)}, f32[16]{0:T(128)}, u32[]{:S(2)}) copy-start(f32[16]{0:T(128)} %skip_ref.1) | copy-start | bytes 196
  46.2 7.3 %collective-permute-start.14 = (f32[128,128]{1,0:T(8,128)S(1)}, f32[128,128]{1,0:T(8,128)S(1)}, u32[]{:S(2)}, u32[]{:S(2)}) collective-permute-start(f32[128,128]{1,0:T(8,128)S(1)} %get-tuple-element.52), channel_id=1, source_target_pairs={{0,4},{4,0},{8,12},{12,8},{16,20},{20,16},{24,28},{28,24},{1,5},{5... | collective-permute-start | bytes 196616 | tf_op jit(solution)/shard_map/ppermute | solution.py:342
  47.6 7.7 %collective-permute-start.15 = (f32[128,128]{1,0:T(8,128)S(1)}, f32[128,128]{1,0:T(8,128)S(1)}, u32[]{:S(2)}, u32[]{:S(2)}) collective-permute-start(f32[128,128]{1,0:T(8,128)S(1)} %get-tuple-element.53), channel_id=1, source_target_pairs={{0,8},{4,12},{8,0},{12,4},{16,24},{20,28},{24,16},{28,20},{1,9},{5... | collective-permute-start | bytes 196616 | tf_op jit(solution)/shard_map/ppermute | solution.py:342
  49.2 9.4 %collective-permute-start.16 = (f32[128,128]{1,0:T(8,128)S(1)}, f32[128,128]{1,0:T(8,128)S(1)}, u32[]{:S(2)}, u32[]{:S(2)}) collective-permute-start(f32[128,128]{1,0:T(8,128)S(1)} %get-tuple-element.54), channel_id=1, source_target_pairs={{0,12},{4,8},{8,4},{12,0},{16,28},{20,24},{24,20},{28,16},{1,13},{... | collective-permute-start | bytes 196616 | tf_op jit(solution)/shard_map/ppermute | solution.py:342
  50.3 9.9 %collective-permute-start.17 = (f32[128,128]{1,0:T(8,128)S(1)}, f32[128,128]{1,0:T(8,128)S(1)}, u32[]{:S(2)}, u32[]{:S(2)}) collective-permute-start(f32[128,128]{1,0:T(8,128)S(1)} %get-tuple-element.55), channel_id=1, source_target_pairs={{0,16},{4,20},{8,24},{12,28},{16,0},{20,4},{24,8},{28,12},{1,17},{... | collective-permute-start | bytes 196616 | tf_op jit(solution)/shard_map/ppermute | solution.py:342
  52.1 10.4 %collective-permute-start.18 = (f32[128,128]{1,0:T(8,128)S(1)}, f32[128,128]{1,0:T(8,128)S(1)}, u32[]{:S(2)}, u32[]{:S(2)}) collective-permute-start(f32[128,128]{1,0:T(8,128)S(1)} %get-tuple-element.56), channel_id=1, source_target_pairs={{0,20},{4,16},{8,28},{12,24},{16,4},{20,0},{24,12},{28,8},{1,21},{... | collective-permute-start | bytes 196616 | tf_op jit(solution)/shard_map/ppermute | solution.py:342
  53.5 9.1 %collective-permute-start.19 = (f32[128,128]{1,0:T(8,128)S(1)}, f32[128,128]{1,0:T(8,128)S(1)}, u32[]{:S(2)}, u32[]{:S(2)}) collective-permute-start(f32[128,128]{1,0:T(8,128)S(1)} %get-tuple-element.57), channel_id=1, source_target_pairs={{0,24},{4,28},{8,16},{12,20},{16,8},{20,12},{24,0},{28,4},{1,25},{... | collective-permute-start | bytes 196616 | tf_op jit(solution)/shard_map/ppermute | solution.py:342
  55.3 7.2 %collective-permute-start.20 = (f32[128,128]{1,0:T(8,128)S(1)}, f32[128,128]{1,0:T(8,128)S(1)}, u32[]{:S(2)}, u32[]{:S(2)}) collective-permute-start(f32[128,128]{1,0:T(8,128)S(1)} %get-tuple-element.58), channel_id=1, source_target_pairs={{0,28},{4,24},{8,20},{12,16},{16,12},{20,8},{24,4},{28,0},{1,29},{... | collective-permute-start | bytes 196616 | tf_op jit(solution)/shard_map/ppermute | solution.py:342
